TPU v7x, 256 devices: a whole 4x4x8 slice. The times are simulated.
256 devices in a mesh: layer: 2 (over core), ex: 128 (over z, y, x).
Axes of the slice: x: 4, y: 4, z: 8, core: 2. Of those that a mesh axis runs over, the one named last changes fastest.
Arguments:
- train_sketch: bfloat16 [12, 65536, 256], P('layer', 'ex')
- val_sketch: bfloat16 [12, 4096, 256], P('layer', 'ex')
- first_moment: float32 [12, 256], P('layer'), may hold values from -0.6 to 0.6
- second_moment: float32 [12, 256], P('layer'), may hold values from 0.01 to 1
- train_pair: int32 [65536], P('ex'), may hold values from 0 to 15
- val_pair: int32 [4096], P('ex'), may hold values from 0 to 15
- block_mask: int32 [16, 16], replicated, may hold values 0 or 1
Outputs:
- scores: bfloat16 [32768, 2, 4096], P('ex', 'layer')
All inputs are finite; a program needn't handle non-finite values.
Results may differ from a plain program's by a relative error of at most 0.0058.
Values may be sent and summed in bfloat16 or wider, within the bound.
No kernel may reach another device: no remote copies, remote signals or barrier semaphores. Data moves between devices by JAX's collectives and lax.ppermute only.
A program may use at most 128 MiB of HBM per device.

v0:
```python
import jax
import jax.numpy as jnp
from jax import lax
from jax.sharding import PartitionSpec as P


def precondition(grad, first_moment, second_moment):
    return (0.9 * first_moment[:, None, :] + 0.1 * grad) / (
        jnp.sqrt(0.999 * second_moment[:, None, :] + 0.001 * grad * grad) + 1e-08
    )


def squares(values):
    return jnp.sum(values * values, axis=(0, 2))


def unit_rows(values, total_sq, scale_factor):
    return (values * (scale_factor * lax.rsqrt(total_sq + 1e-06))[None, :, None]).astype(
        jnp.bfloat16
    )


def contract(left, right):
    return lax.dot_general(
        left, right, (((0, 2), (0, 2)), ((), ())), preferred_element_type=jnp.float32
    )


def local(train_sketch, val_sketch, first_moment, second_moment, train_pair, val_pair, block_mask):
    lay_dev, tr_ex, width = train_sketch.shape
    layer_count = lax.axis_size("layer")
    rows_here = tr_ex // layer_count
    scale_factor = float(lay_dev * layer_count * width) ** 0.25
    pair_count = block_mask.shape[0]
    labels = jnp.arange(pair_count, dtype=jnp.int32)
    val_all = lax.all_gather(val_sketch, "ex", axis=1, tiled=True)
    val_labels = lax.all_gather(val_pair, "ex", axis=0, tiled=True)
    val_onehot = (labels[:, None] == val_labels[None, :]).astype(jnp.bfloat16)
    pairs_here = lax.dynamic_slice_in_dim(
        train_pair, lax.axis_index("layer") * rows_here, rows_here, 0
    )
    mine = lax.all_to_all(train_sketch, "layer", split_axis=1, concat_axis=0, tiled=True)
    first_all, second_all = (
        lax.all_gather(first_moment, "layer", axis=0, tiled=True),
        lax.all_gather(second_moment, "layer", axis=0, tiled=True),
    )
    val_full = lax.all_gather(val_all, "layer", axis=0, tiled=True)
    pre = precondition(mine.astype(jnp.float32), first_all, second_all)
    unit_train = unit_rows(pre, squares(pre), scale_factor)
    val_float = val_full.astype(jnp.float32)
    unit_val = unit_rows(val_float, squares(val_float), scale_factor)
    raw = contract(unit_train, unit_val)
    train_onehot = (pairs_here[:, None] == labels[None, :]).astype(jnp.bfloat16)
    row_mask = jnp.dot(
        train_onehot, block_mask.astype(jnp.bfloat16), preferred_element_type=jnp.float32
    ).astype(jnp.bfloat16)
    weights = jnp.dot(row_mask, val_onehot, preferred_element_type=jnp.float32)
    return (raw * weights).astype(jnp.bfloat16)[:, None, :]


def solution(mesh):
    placed = (
        P("layer", "ex", None),
        P("layer", "ex", None),
        P("layer", None),
        P("layer", None),
        P("ex"),
        P("ex"),
        P(),
    )
    return jax.shard_map(
        local, mesh=mesh, in_specs=placed, out_specs=P("ex", "layer", None), check_vma=False
    )
```

profile of v0, /device:TPU:0, one launch (start us, length us, event | category | flops | bytes accessed | tf_op | source)
XLA Modules:
  0.0 894.7 jit_solution(7352749476020731532)
XLA Ops:
  6.5 0.0 all-gather.5.cloned.1.call-start
  6.5 0.7 all-gather.5.cloned.1.call-update
  7.3 0.0 all-gather.7.cloned.1.call-start
  7.3 143.9 %all-gather.5.cloned.1.call-done = bf16[6,4096,256]{2,1,0:T(8,128)(2,1)} async-done(((bf16[6,32,256]{2,1,0:T(8,128)(2,1)}), bf16[6,4096,256]{2,1,0:T(8,128)(2,1)}) %all-gather.5.cloned.1.call-update) | async-done | bytes 12582928 | tf_op jit(solution)/shard_map/all_gather | solution.py:36
  151.2 0.0 copy-start
  151.2 0.0 all-gather.7.cloned.1.call-update
  151.2 1.4 copy-done
  152.6 0.0 copy-start.2
  152.6 0.0 copy-start.3
  152.6 2.2 copy.14
  154.9 3.8 all-to-all-start
  158.6 0.0 copy-done.2
  158.6 2.6 all-gather
  161.3 0.0 copy-done.3
  161.3 1.8 all-gather.1
  163.1 0.0 all-to-all-done
  163.1 0.3 convert_bitcast_fusion
  163.5 0.0 copy-start.6
  163.5 0.0 copy-start.4
  163.5 0.0 copy-start.5
  163.5 3.4 copy.15
  166.9 0.0 copy-done.6
  166.9 0.6 dynamic-slice
  168.1 0.0 copy-done.4
  168.1 0.1 dynamic_slice.3
  168.2 0.0 copy-done.5
  168.2 0.2 dynamic-update-slice
  168.5 684.9 %all-reduce = s32[4096]{0:T(1024)S(1)} all-reduce(s32[4096]{0:T(1024)S(1)} %dynamic-update-slice), channel_id=1, replica_groups=mesh['layer'=2,'ex'=128] {'ex'}, use_global_device_ids=true, to_apply=%add | all-reduce | flops 4096 | bytes 32768
  853.4 2.9 fusion.15
  856.3 3.6 fusion.22
  859.9 0.0 all-gather.7.cloned.1.call-done
  859.9 10.3 %fusion = f32[4096]{0:T(1024)S(1)} fusion(bf16[12,4096,256]{2,1,0:T(8,128)(2,1)} %all-gather.7.cloned.1.call-done), kind=kLoop, calls=%fused_computation.2 | loop fusion | flops 37744640 | bytes 25182208 | tf_op jit(solution)/shard_map/reduce_sum | solution.py:14
  870.3 0.0 copy-start.1
  870.3 13.1 %fusion.5 = f32[256,4096]{1,0:T(8,128)} fusion(bf16[12,256,256]{2,1,0:T(8,128)(2,1)S(1)} %fusion.22, bf16[12,4096,256]{2,1,0:T(8,128)(2,1)} %all-gather.7.cloned.1.call-done, f32[4096]{0:T(1024)S(1)} %rsqrt_multiply_fusion), kind=kOutput, calls=%fused_computation.7 | convolution fusion | flops 6480199680 | bytes 30949376 | tf_op jit(solution)/shard_map/dot_general | solution.py:24
  883.4 0.0 copy-done.1
  883.4 4.5 fusion.9
  (7 shorter events, 0.0 us)
Async XLA Ops:
  6.5 144.7 %all-gather.5.cloned.1.call-start = ((), (), s32[]{:S(2)}) async-start(), calls=%async_computation.1 | async-start | bytes 12681216 | tf_op jit(solution)/shard_map/all_gather | solution.py:36
  7.3 852.7 %all-gather.7.cloned.1.call-start = ((), (), s32[]{:S(2)}) async-start(), calls=%async_computation.2 | async-start | bytes 37748736 | tf_op jit(solution)/shard_map/all_gather | solution.py:47
  151.2 1.4 copy-start
  152.6 6.0 copy-start.2
  152.6 8.7 copy-start.3
  154.9 8.3 all-to-all-start
  163.5 3.4 copy-start.6
  163.5 4.7 copy-start.4
  163.5 4.7 copy-start.5
  870.3 13.1 %copy-start.1 = (s32[16,16]{1,0:T(8,128)S(1)}, s32[16,16]{1,0:T(8,128)}, u32[]{:S(2)}) copy-start(s32[16,16]{1,0:T(8,128)} %param.13) | copy-start | bytes 3076
Sparse Core Ops, SparseCore 0:
  10.9 140.2 all-gather.4
  153.0 42.9 all-gather.6
where the time goes:
time: 895 us
  blocking collectives  689 us (77%)
  waiting for transfers between devices  145 us (16%)
  matrix products  17.6 us (2%)
  other arithmetic  17.2 us (2%)
  between operations  14.2 us (2%)
    unnamed x1, blocking collectives  685 us
    all_gather x1, waiting for transfers between devices, local(): val_all = lax.all_gather(val_sketch, 'ex', axis=1, tiled=True)  144 us
  transfers between devices with their start and end apart: 3, of which 1 were waited for; matrix products, arithmetic and copies ran while one was open for 1% of the time, Pallas kernels for 0%

commit v1 on v0

v1 whole, which is shorter than its diff:
```python
import jax
import jax.numpy as jnp
from jax import lax
from jax.experimental import pallas as pl
from jax.experimental.pallas import tpu as pltpu
from jax.sharding import PartitionSpec as P

SWAP = [(0, 1), (1, 0)]
NT = (((1,), (1,)), ((), ()))
NN = (((1,), (0,)), ((), ()))


def other(x):
    return lax.ppermute(x, "layer", SWAP)


def precondition(grad, first_moment, second_moment):
    return (0.9 * first_moment[:, None, :] + 0.1 * grad) / (
        jnp.sqrt(0.999 * second_moment[:, None, :] + 0.001 * grad * grad) + 1e-08
    )


def unit_rows(values, scale_factor):
    total_sq = jnp.sum(values * values, axis=(0, 2))
    return (values * (scale_factor * lax.rsqrt(total_sq + 1e-06))[None, :, None]).astype(
        jnp.bfloat16
    )


def pack_kernel(lay_ref, pair_ref, val_ref, recv_ref, out_ref):
    layers, both, width = val_ref.shape
    mine = both // 2
    first = pl.multiple_of(lay_ref[0] * mine, mine)
    pieces = [val_ref[l, pl.ds(first, mine), :] for l in range(layers)]
    pieces += [recv_ref[l] for l in range(layers)]
    pieces = [piece.astype(jnp.float32) for piece in pieces]
    total_sq = sum(jnp.sum(piece * piece, axis=1, keepdims=True) for piece in pieces)
    scale = float(2 * layers * width) ** 0.25 * lax.rsqrt(total_sq + 1e-06)
    for l, piece in enumerate(pieces):
        out_ref[:, l * width : (l + 1) * width] = (piece * scale).astype(out_ref.dtype)
    row = lax.broadcasted_iota(jnp.int32, (mine, 128), 0)
    label = jnp.zeros((mine, 128), jnp.int32)
    for r in range(mine):
        label = jnp.where(row == r, pair_ref[first + r], label)
    lane = lax.broadcasted_iota(jnp.int32, (mine, 128), 1)
    out_ref[:, 2 * layers * width :] = jnp.where(label == lane, 1.0, 0.0).astype(out_ref.dtype)


def pack(lay, val_pair, val_sketch, recv):
    layers, both, width = val_sketch.shape
    return pl.pallas_call(
        pack_kernel,
        grid_spec=pltpu.PrefetchScalarGridSpec(
            num_scalar_prefetch=2,
            grid=(1,),
            in_specs=[
                pl.BlockSpec(val_sketch.shape, lambda i, *s: (0, 0, 0)),
                pl.BlockSpec(recv.shape, lambda i, *s: (0, 0, 0)),
            ],
            out_specs=pl.BlockSpec((both // 2, 2 * layers * width + 128), lambda i, *s: (0, 0)),
        ),
        out_shape=jax.ShapeDtypeStruct((both // 2, 2 * layers * width + 128), jnp.bfloat16),
        name="pack",
    )(lay, val_pair, val_sketch, recv)


def score_kernel(lay_ref, a_ref, m_ref, b_ref, own_ref, oth_ref):
    layers, rows, width = a_ref.shape
    half = rows // 2
    depth = layers * width
    lay = lay_ref[0]
    for which, out_ref in ((lay, own_ref), (1 - lay, oth_ref)):
        part = pl.ds(pl.multiple_of(which * half, half), half)
        left = jnp.concatenate([a_ref[l, part, :] for l in range(layers)], axis=1)
        raw = lax.dot_general(
            left, b_ref[:, :depth], NT, preferred_element_type=jnp.float32
        )
        weight = lax.dot_general(
            m_ref[part, :], b_ref[:, depth:], NT, preferred_element_type=jnp.float32
        )
        out_ref[...] = (raw * weight).astype(out_ref.dtype)


def score(lay, a, row_mask, b, tile):
    layers, rows, width = a.shape
    cols, wide = b.shape
    shape = jax.ShapeDtypeStruct((rows // 2, cols), jnp.bfloat16)
    return pl.pallas_call(
        score_kernel,
        grid_spec=pltpu.PrefetchScalarGridSpec(
            num_scalar_prefetch=1,
            grid=(cols // tile,),
            in_specs=[
                pl.BlockSpec((layers, rows, width), lambda j, s: (0, 0, 0)),
                pl.BlockSpec(row_mask.shape, lambda j, s: (0, 0)),
                pl.BlockSpec((tile, wide), lambda j, s: (j, 0)),
            ],
            out_specs=[pl.BlockSpec((rows // 2, tile), lambda j, s: (0, j))] * 2,
        ),
        out_shape=[shape, shape],
        compiler_params=pltpu.CompilerParams(vmem_limit_bytes=48 << 20),
        name="score",
    )(lay, a, row_mask, b)


def place_kernel(own_ref, recv_ref, spread_ref, out_ref):
    both = jnp.concatenate([own_ref[...], recv_ref[...]], axis=1)
    out_ref[...] = lax.dot_general(
        both, spread_ref[...], NN, preferred_element_type=jnp.float32
    ).astype(out_ref.dtype)


def place(own, recv, spread, tile):
    rows, cols = own.shape
    return pl.pallas_call(
        place_kernel,
        grid=(cols // tile,),
        in_specs=[
            pl.BlockSpec((rows, tile), lambda j: (0, j)),
            pl.BlockSpec((rows, tile), lambda j: (0, j)),
            pl.BlockSpec((2 * tile, 2 * tile), lambda j: (0, 0)),
        ],
        out_specs=pl.BlockSpec((rows, 2 * tile), lambda j: (0, j)),
        out_shape=jax.ShapeDtypeStruct((rows, 2 * cols), jnp.bfloat16),
        name="place",
    )(own, recv, spread)


def local(train_sketch, val_sketch, first_moment, second_moment, train_pair, val_pair, block_mask):
    lay_dev, tr_ex, width = train_sketch.shape
    val_ex = val_sketch.shape[1]
    mine = val_ex // 2
    lay = lax.axis_index("layer")
    scale_factor = float(2 * lay_dev * width) ** 0.25
    pairs = block_mask.shape[0]
    labels = jnp.arange(128, dtype=jnp.int32)

    give = lax.dynamic_slice_in_dim(val_sketch, (1 - lay) * mine, mine, 1)
    payload = pack(lay[None], val_pair, val_sketch, other(give))
    everyone = lax.all_gather(payload, "ex", axis=0, tiled=True)

    train = jnp.concatenate([train_sketch, other(train_sketch)], axis=0)
    moments = jnp.stack([first_moment, second_moment])
    moments = jnp.concatenate([moments, other(moments)], axis=1)
    pre = precondition(train.astype(jnp.float32), moments[0], moments[1])
    unit_train = unit_rows(pre, scale_factor)
    train_onehot = (train_pair[:, None] == labels[None, :pairs]).astype(jnp.bfloat16)
    wide_mask = jnp.pad(block_mask.astype(jnp.bfloat16), ((0, 0), (0, 128 - pairs)))
    row_mask = jnp.dot(train_onehot, wide_mask, preferred_element_type=jnp.float32).astype(
        jnp.bfloat16
    )

    own, oth = score(lay[None], unit_train, row_mask, everyone, 256)
    recv = other(oth)
    tile = 128
    at = jnp.arange(tile, dtype=jnp.int32)
    base = (at // mine) * val_ex + at % mine
    target = jnp.concatenate([base + lay * mine, base + (1 - lay) * mine])
    spread = (target[:, None] == jnp.arange(2 * tile, dtype=jnp.int32)[None, :]).astype(
        jnp.bfloat16
    )
    return place(own, recv, spread, tile)[:, None, :]


def solution(mesh):
    placed = (
        P("layer", "ex", None),
        P("layer", "ex", None),
        P("layer", None),
        P("layer", None),
        P("ex"),
        P("ex"),
        P(),
    )
    return jax.shard_map(
        local, mesh=mesh, in_specs=placed, out_specs=P("ex", "layer", None), check_vma=False
    )
```

time: 895 us -> 189 us (0.21)
  the two profiles are of different devices: /device:TPU:0 before, /device:TPU:1 now
where the time goes in v1:
time: 189 us; the launch traced here: 188 us
  waiting for transfers between devices  128 us (68%)
  Pallas kernels  24.9 us (13%)
  between operations  13.4 us (7%)
  other arithmetic  12.8 us (7%)
  starting transfers between devices  4.83 us (3%)
  local copies, waits for them, and re-layouts  3.4 us (2%)
    all_gather x1, waiting for transfers between devices, local(): everyone = lax.all_gather(payload, 'ex', axis=0, tiled=True)  125 us
    pallas_call x1, Pallas kernels, score(): pl.pallas_call(score_kernel, grid_spec=pltpu.PrefetchScalarGridSpec(num_s...  12.1 us
    pallas_call x1, Pallas kernels, place(): pl.pallas_call(place_kernel, grid=(cols // tile,), in_specs=[pl.BlockSpec...  10.5 us
    reduce_sum x1, other arithmetic, unit_rows(): total_sq = jnp.sum(values * values, axis=(0, 2))  4.95 us
    convert_element_type x1, other arithmetic, unit_rows(): (values * (scale_factor * lax.rsqrt(total_sq + 1e-06))[None, :, None]).as...  4.89 us
    ppermute x4, starting transfers between devices, other(): return lax.ppermute(x, 'layer', SWAP)  4.83 us
  transfers between devices with their start and end apart: 5, of which 4 were waited for; matrix products, arithmetic and copies ran while one was open for 7% of the time, Pallas kernels for 0%

profile of v1, /device:TPU:1, one launch (start us, length us, event | category | flops | bytes accessed | tf_op | source)
XLA Modules:
  0.0 188.3 jit_solution(13922842047107063994)
XLA Ops:
  6.5 0.0 all-gather.2.cloned.1.call-start
  6.5 0.8 constant_dynamic-slice_fusion
  7.3 3.2 %collective-permute-start.2 = (bf16[6,16,256]{2,1,0:T(8,128)(2,1)S(1)}, bf16[6,16,256]{2,1,0:T(8,128)(2,1)S(1)}, u32[]{:S(2)}, u32[]{:S(2)}) collective-permute-start(bf16[6,16,256]{2,1,0:T(8,128)(2,1)S(1)} %constant_dynamic-slice_fusion), channel_id=1, source_target_pairs={{0,128},{128,0},{1,129},{129,1},{2,130},{130,2},{3,131},{131,3},{4... | collective-permute-start | bytes 147464 | tf_op jit(solution)/shard_map/ppermute | solution.py:14
  10.6 0.9 collective-permute-done.2.recv_ref
  11.5 0.0 copy-start.2
  11.5 0.6 copy-done.2
  12.1 2.3 %pack.1 = bf16[16,3200]{1,0:T(8,128)(2,1)} custom-call(s32[1]{0:T(128)} %bitcast.lay_ref, s32[32]{0:T(128)} %pair_ref.1, bf16[6,32,256]{2,1,0:T(8,128)(2,1)} %val_ref.1, bf16[6,16,256]{2,1,0:T(8,128)(2,1)} %copy-done.2), custom_call_target="tpu_custom_call" | custom-call | tf_op jit(solution)/shard_map/pack/pallas_call | solution.py:51
  14.4 0.0 all-gather.2.cloned.1.call-update
  14.4 0.4 collective-permute-start.1
  14.9 0.7 pad_maximum_fusion.1
  15.6 0.2 collective-permute-start
  15.7 0.7 convert_element_type.20
  16.4 0.9 convolution_convert_fusion.m_ref
  17.4 0.6 collective-permute-done
  18.0 0.7 pad_maximum_fusion
  18.7 0.0 collective-permute-done.1
  18.7 5.0 %multiply_reduce_fusion = f32[512]{0:T(512)S(1)} fusion(f32[12,256]{1,0:T(8,128)S(1)} %get-tuple-element.10, bf16[6,512,256]{2,1,0:T(8,128)(2,1)S(1)} %collective-permute-done.1, bf16[6,512,256]{2,1,0:T(8,128)(2,1)} %param.7, f32[12,256]{1,0:T(8,128)S(1)} %get-tuple-element.9), kind=kLoop, calls=%fused_computation.8 | loop fusion | flops 17300992 | bytes 3172352 | tf_op jit(solution)/shard_map/reduce_sum | solution.py:24
  23.7 4.9 %multiply_convert_fusion.a_ref = bf16[12,512,256]{2,1,0:T(8,128)(2,1)S(1)} fusion(f32[512]{0:T(512)S(1)} %rsqrt_multiply_fusion, f32[12,256]{1,0:T(8,128)S(1)} %get-tuple-element.10, bf16[6,512,256]{2,1,0:T(8,128)(2,1)S(1)} %collective-permute-done.1, bf16[6,512,256]{2,1,0:T(8,128)(2,1)} %param.7, f32[12,256]{1,0:T(8,128)S(1)} %get-tuple-element.9), kind=kLoop, calls=%fused_computation.7 | loop fusion | flops 17301504 | bytes 6318080 | tf_op jit(solution)/shard_map/convert_element_type | solution.py:25
  28.6 124.9 %all-gather.2.cloned.1.call-done.b_ref = bf16[2048,3200]{1,0:T(8,128)(2,1)} async-done(((bf16[16,3200]{1,0:T(8,128)(2,1)}), bf16[2048,3200]{1,0:T(8,128)(2,1)}) %all-gather.2.cloned.1.call-update) | async-done | bytes 13107216 | tf_op jit(solution)/shard_map/all_gather | solution.py:140
  153.5 12.1 %score.1 = (bf16[256,2048]{1,0:T(8,128)(2,1)S(1)}, bf16[256,2048]{1,0:T(8,128)(2,1)}) custom-call(s32[1]{0:T(128)} %bitcast.lay_ref, bf16[12,512,256]{2,1,0:T(8,128)(2,1)S(1)} %multiply_convert_fusion.a_ref, bf16[512,128]{1,0:T(8,128)(2,1)S(1)} %convolution_convert_fusion.m_ref, bf16[2048,3200]{1,0:T(8,128)(2,1)} %all-gather.2.cloned.1.call-done.b_ref), custom_call_target="tpu_custom_call" | custom-call | tf_op jit(solution)/shard_map/score/pallas_call | solution.py:88
  165.5 0.0 copy-start
  165.5 1.0 copy-done
  166.5 1.0 collective-permute-start.3
  167.5 0.8 fusion.5.spread_ref
  168.3 1.7 collective-permute-done.3.recv_ref
  170.0 0.0 copy-start.1
  170.0 1.0 copy-done.1
  171.0 10.5 %place.1 = bf16[256,4096]{1,0:T(8,128)(2,1)} custom-call(bf16[256,2048]{1,0:T(8,128)(2,1)} %copy-done, bf16[256,2048]{1,0:T(8,128)(2,1)} %copy-done.1, bf16[256,256]{1,0:T(8,128)(2,1)} %fusion.5.spread_ref), custom_call_target="tpu_custom_call" | custom-call | tf_op jit(solution)/shard_map/place/pallas_call | solution.py:115
  (6 shorter events, 0.0 us)
Async XLA Ops:
  6.5 146.9 %all-gather.2.cloned.1.call-start = ((), (), s32[]{:S(2)}) async-start(), calls=%async_computation | async-start | bytes 13209600 | tf_op jit(solution)/shard_map/all_gather | solution.py:140
  7.3 4.1 %collective-permute-start.2 = (bf16[6,16,256]{2,1,0:T(8,128)(2,1)S(1)}, bf16[6,16,256]{2,1,0:T(8,128)(2,1)S(1)}, u32[]{:S(2)}, u32[]{:S(2)}) collective-permute-start(bf16[6,16,256]{2,1,0:T(8,128)(2,1)S(1)} %constant_dynamic-slice_fusion), channel_id=1, source_target_pairs={{0,128},{128,0},{1,129},{129,1},{2,130},{130,2},{3,131},{131,3},{4... | collective-permute-start | bytes 147464 | tf_op jit(solution)/shard_map/ppermute | solution.py:14
  11.5 0.6 copy-start.2
  14.4 4.3 %collective-permute-start.1 = (bf16[6,512,256]{2,1,0:T(8,128)(2,1)}, bf16[6,512,256]{2,1,0:T(8,128)(2,1)S(1)}, u32[]{:S(2)}, u32[]{:S(2)}) collective-permute-start(bf16[6,512,256]{2,1,0:T(8,128)(2,1)} %param.7), channel_id=1, source_target_pairs={{0,128},{128,0},{1,129},{129,1},{2,130},{130,2},{3,131},{131,3},{4... | collective-permute-start | bytes 4718600 | tf_op jit(solution)/shard_map/ppermute | solution.py:14
  15.6 2.4 %collective-permute-start = (f32[2,6,256]{2,1,0:T(8,128)S(1)}, f32[2,6,256]{2,1,0:T(8,128)S(1)}, u32[]{:S(2)}, u32[]{:S(2)}) collective-permute-start(f32[2,6,256]{2,1,0:T(8,128)S(1)} %pad_maximum_fusion.1), channel_id=1, source_target_pairs={{0,128},{128,0},{1,129},{129,1},{2,130},{130,2},{3,131},{131,3},{4... | collective-permute-start | bytes 36872 | tf_op jit(solution)/shard_map/ppermute | solution.py:14
  165.5 1.0 copy-start
  166.5 3.5 %collective-permute-start.3 = (bf16[256,2048]{1,0:T(8,128)(2,1)}, bf16[256,2048]{1,0:T(8,128)(2,1)S(1)}, u32[]{:S(2)}, u32[]{:S(2)}) collective-permute-start(bf16[256,2048]{1,0:T(8,128)(2,1)} %get-tuple-element.8), channel_id=1, source_target_pairs={{0,128},{128,0},{1,129},{129,1},{2,130},{130,2},{3,131},{131,3},{4... | collective-permute-start | bytes 3145736 | tf_op jit(solution)/shard_map/ppermute | solution.py:14
  170.0 1.0 copy-start.1
Sparse Core Ops, SparseCore 0:
  14.6 138.8 all-gather.1

commit v2 on v1

--- a/solution.py
+++ b/solution.py
@@ -64,66 +64,205 @@
     )(lay, val_pair, val_sketch, recv)
 
 
-def score_kernel(lay_ref, a_ref, m_ref, b_ref, own_ref, oth_ref):
+SIZE = {"z": 8, "y": 4, "x": 4}
+RING8 = (0, -1, 1, -2, 2, -3, 3, 4)
+RING4 = (0, -1, 1, 2)
+C_COLUMNS = 1152
+
+
+def shifted(axis, step):
+    chips = []
+    for chip in range(128):
+        at = {"z": chip // 16, "y": chip // 4 % 4, "x": chip % 4}
+        at[axis] = (at[axis] + step) % SIZE[axis]
+        chips.append(at["z"] * 16 + at["y"] * 4 + at["x"])
+    return chips
+
+
+def send(block, axes, step):
+    pairs = [
+        (128 * core + chip, 128 * core + there)
+        for core in (0, 1)
+        for chip, there in enumerate(shifted(axes[core], step))
+    ]
+    return lax.ppermute(block, ("layer", "ex"), pairs)
+
+
+def around8(block):
+    half = block.shape[0] // 2
+    up = down = block
+    found = [block]
+    for _ in range(3):
+        up, down = send(up, "zz", 1), send(down, "zz", -1)
+        found += [up, down]
+    return found, (send(up[:half], "zz", 1), send(down[half:], "zz", -1))
+
+
+def straight4(block, axes):
+    return jnp.concatenate([block] + [send(block, axes, step) for step in (1, -1, 2)], axis=0)
+
+
+def around4(block, axes):
+    half = block.shape[0] // 2
+    up, down = send(block, axes, 1), send(block, axes, -1)
+    return up, down, send(up[:half], axes, 1), send(down[half:], axes, -1)
+
+
+def both_halves(s_ref, a_ref, m_ref, d, c, own_ref, oth_ref, cols):
     layers, rows, width = a_ref.shape
     half = rows // 2
-    depth = layers * width
-    lay = lay_ref[0]
+    depth = d.shape[1]
+    lay = s_ref[0]
     for which, out_ref in ((lay, own_ref), (1 - lay, oth_ref)):
         part = pl.ds(pl.multiple_of(which * half, half), half)
         left = jnp.concatenate([a_ref[l, part, :] for l in range(layers)], axis=1)
-        raw = lax.dot_general(
-            left, b_ref[:, :depth], NT, preferred_element_type=jnp.float32
+        raw = lax.dot_general(left[:, :depth], d, NT, preferred_element_type=jnp.float32)
+        raw += lax.dot_general(left[:, depth:], c[:, :-128], NT, preferred_element_type=jnp.float32)
+        weight = lax.dot_general(
+            m_ref[part, :], c[:, -128:], NT, preferred_element_type=jnp.float32
         )
-        weight = lax.dot_general(
-            m_ref[part, :], b_ref[:, depth:], NT, preferred_element_type=jnp.float32
-        )
-        out_ref[...] = (raw * weight).astype(out_ref.dtype)
-
-
-def score(lay, a, row_mask, b, tile):
+        out_ref[:, cols] = (raw * weight).astype(out_ref.dtype)
+
+
+def early_kernel(s_ref, a_ref, m_ref, *refs):
+    d_refs, c_refs = refs[:3], refs[3:12]
+    own_ref, oth_ref, late_ref, c_all = refs[12:]
+    step = pl.program_id(0)
+
+    for k in range(7):
+
+        @pl.when(step == k)
+        def _():
+            c_all[...] = c_refs[k][...]
+
+    @pl.when(step == 7)
+    def _():
+        near = c_refs[7].shape[0]
+        c_all[:near] = c_refs[7][...]
+        c_all[near:] = c_refs[8][...]
+
+    d = jnp.concatenate([ref[...].reshape(-1, ref.shape[-1]) for ref in d_refs], axis=0)
+    cut = d.shape[0]
+    both_halves(s_ref, a_ref, m_ref, d, c_all[:cut], own_ref, oth_ref, slice(0, cut))
+    for ref in (own_ref, oth_ref):
+        ref[:, cut:] = jnp.zeros((ref.shape[0], ref.shape[1] - cut), ref.dtype)
+    late_ref[...] = c_all[cut:]
+
+
+def whole(block):
+    return pl.BlockSpec(block.shape, lambda *_: (0,) * block.ndim, pipeline_mode=pl.Buffered(1))
+
+
+def early_score(lay, a, row_mask, d_blocks, c_blocks):
     layers, rows, width = a.shape
-    cols, wide = b.shape
-    shape = jax.ShapeDtypeStruct((rows // 2, cols), jnp.bfloat16)
+    cols = c_blocks[0].shape[0]
+    c_wide = c_blocks[0].shape[1]
+    late = cols // 4
+    shape = jax.ShapeDtypeStruct((rows // 2, 8 * cols), jnp.bfloat16)
+
+    def d_spec(block):
+        return pl.BlockSpec((block.shape[0], None) + block.shape[2:], lambda j, s: (0, j, 0, 0))
+
     return pl.pallas_call(
-        score_kernel,
+        early_kernel,
         grid_spec=pltpu.PrefetchScalarGridSpec(
             num_scalar_prefetch=1,
-            grid=(cols // tile,),
-            in_specs=[
-                pl.BlockSpec((layers, rows, width), lambda j, s: (0, 0, 0)),
-                pl.BlockSpec(row_mask.shape, lambda j, s: (0, 0)),
-                pl.BlockSpec((tile, wide), lambda j, s: (j, 0)),
-            ],
-            out_specs=[pl.BlockSpec((rows // 2, tile), lambda j, s: (0, j))] * 2,
+            grid=(8,),
+            in_specs=[whole(a), whole(row_mask)]
+            + [d_spec(block) for block in d_blocks]
+            + [whole(block) for block in c_blocks],
+            out_specs=[pl.BlockSpec((rows // 2, cols), lambda j, s: (0, j))] * 2
+            + [pl.BlockSpec((late, c_wide), lambda j, s: (j, 0))],
+            scratch_shapes=[pltpu.VMEM((cols, c_wide), jnp.bfloat16)],
         ),
+        out_shape=[shape, shape, jax.ShapeDtypeStruct((8 * late, c_wide), jnp.bfloat16)],
+        compiler_params=pltpu.CompilerParams(vmem_limit_bytes=56 << 20),
+        cost_estimate=pl.CostEstimate(
+            flops=2 * rows * 6 * cols * layers * width, bytes_accessed=30 << 20, transcendentals=0
+        ),
+        name="early_score",
+    )(lay, a, row_mask, *d_blocks, *c_blocks)
+
+
+def late_kernel(s_ref, a_ref, m_ref, near_ref, far_ref, c_ref, own_ref, oth_ref):
+    pieces = []
+    for j in range(near_ref.shape[1]):
+        for ref in (near_ref, far_ref):
+            pieces += [ref[i, j] for i in range(ref.shape[0])]
+    d = jnp.concatenate(pieces, axis=0)
+    both_halves(s_ref, a_ref, m_ref, d, c_ref[...], own_ref, oth_ref, slice(None))
+
+
+def late_score(lay, a, row_mask, near, far, c):
+    layers, rows, width = a.shape
+    shape = jax.ShapeDtypeStruct((rows // 2, c.shape[0]), jnp.bfloat16)
+    smem = pl.BlockSpec(memory_space=pltpu.SMEM)
+    vmem = pl.BlockSpec(memory_space=pltpu.VMEM)
+    return pl.pallas_call(
+        late_kernel,
+        in_specs=[smem] + [vmem] * 5,
+        out_specs=[vmem] * 2,
         out_shape=[shape, shape],
-        compiler_params=pltpu.CompilerParams(vmem_limit_bytes=48 << 20),
-        name="score",
-    )(lay, a, row_mask, b)
-
-
-def place_kernel(own_ref, recv_ref, spread_ref, out_ref):
-    both = jnp.concatenate([own_ref[...], recv_ref[...]], axis=1)
-    out_ref[...] = lax.dot_general(
-        both, spread_ref[...], NN, preferred_element_type=jnp.float32
-    ).astype(out_ref.dtype)
-
-
-def place(own, recv, spread, tile):
+        compiler_params=pltpu.CompilerParams(vmem_limit_bytes=56 << 20),
+        name="late_score",
+    )(lay, a, row_mask, near, far, c)
+
+
+def place_kernel(depth_ref, own_ref, recv_ref, own2_ref, recv2_ref, spread_ref, out_ref):
+    tile = own_ref.shape[1] // 8
+    for j in range(8):
+        cols = slice(j * tile, (j + 1) * tile)
+        pair = slice(j // 2 * 128, (j // 2 + 1) * 128)
+        both = jnp.concatenate(
+            [own_ref[:, cols], recv_ref[:, cols], own2_ref[:, pair], recv2_ref[:, pair]], axis=1
+        )
+        into = pl.ds(pl.multiple_of(depth_ref[j] * 2 * tile, 2 * tile), 2 * tile)
+        out_ref[:, into] = lax.dot_general(
+            both, spread_ref[j % 2], NN, preferred_element_type=jnp.float32
+        ).astype(out_ref.dtype)
+
+
+def place(depth, own, recv, own2, recv2, spread):
     rows, cols = own.shape
+    vmem = pl.BlockSpec(memory_space=pltpu.VMEM)
     return pl.pallas_call(
         place_kernel,
-        grid=(cols // tile,),
-        in_specs=[
-            pl.BlockSpec((rows, tile), lambda j: (0, j)),
-            pl.BlockSpec((rows, tile), lambda j: (0, j)),
-            pl.BlockSpec((2 * tile, 2 * tile), lambda j: (0, 0)),
-        ],
-        out_specs=pl.BlockSpec((rows, 2 * tile), lambda j: (0, j)),
+        in_specs=[pl.BlockSpec(memory_space=pltpu.SMEM)] + [vmem] * 5,
+        out_specs=vmem,
         out_shape=jax.ShapeDtypeStruct((rows, 2 * cols), jnp.bfloat16),
+        compiler_params=pltpu.CompilerParams(vmem_limit_bytes=56 << 20),
         name="place",
-    )(own, recv, spread)
+    )(depth, own, recv, own2, recv2, spread)
+
+
+def columns(core, chip, mine):
+    at = jnp.arange(256, dtype=jnp.int32)
+    ring = jnp.array(RING4, jnp.int32)
+    first = ring[at // mine % 4]
+    second = ring[at // (4 * mine)]
+    along_x = jnp.where(core == 0, first, second)
+    along_y = jnp.where(core == 0, second, first)
+    x = (chip % 4 + along_x) % 4
+    y = (chip // 4 % 4 + along_y) % 4
+    return (y * 4 + x) * (2 * mine) + core * mine + at % mine
+
+
+def spread_targets(lay, chip, mine):
+    sides = []
+    for core in (lay, 1 - lay):
+        target = columns(core, chip, mine)
+        cut = 12 * mine
+        early = jnp.where(jnp.arange(256) < cut, target, -1)
+        none = jnp.full((4 * mine,), -1, jnp.int32)
+        late = target[cut:]
+        sides.append((early, jnp.concatenate([late, none]), jnp.concatenate([none, late])))
+    (early, even, odd), (early_there, even_there, odd_there) = sides
+    return jnp.stack(
+        [
+            jnp.concatenate([early, early_there, even, even_there]),
+            jnp.concatenate([early, early_there, odd, odd_there]),
+        ]
+    )
 
 
 def local(train_sketch, val_sketch, first_moment, second_moment, train_pair, val_pair, block_mask):
@@ -137,11 +276,24 @@
 
     give = lax.dynamic_slice_in_dim(val_sketch, (1 - lay) * mine, mine, 1)
     payload = pack(lay[None], val_pair, val_sketch, other(give))
-    everyone = lax.all_gather(payload, "ex", axis=0, tiled=True)
-
-    train = jnp.concatenate([train_sketch, other(train_sketch)], axis=0)
+    train = other(train_sketch)
     moments = jnp.stack([first_moment, second_moment])
-    moments = jnp.concatenate([moments, other(moments)], axis=1)
+    moments_there = other(moments)
+    payload, train, moments_there = lax.optimization_barrier((payload, train, moments_there))
+    train = jnp.concatenate([train_sketch, train], axis=0)
+    moments = jnp.concatenate([moments, moments_there], axis=1)
+
+    cut = payload.shape[1] - C_COLUMNS
+    stacks, ends = around8(payload[:, :cut])
+    stack = jnp.concatenate(stacks + list(ends), axis=0)
+    slab = straight4(stack, "xy")
+    d_blocks = [
+        block.reshape(-1, 8, mine, cut) for block in (slab,) + around4(slab, "yx")
+    ]
+    plane = straight4(straight4(payload[:, cut:], "xy"), "yx")
+    planes, ends = around8(plane)
+    c_blocks = planes + list(ends)
+
     pre = precondition(train.astype(jnp.float32), moments[0], moments[1])
     unit_train = unit_rows(pre, scale_factor)
     train_onehot = (train_pair[:, None] == labels[None, :pairs]).astype(jnp.bfloat16)
@@ -150,16 +302,15 @@
         jnp.bfloat16
     )
 
-    own, oth = score(lay[None], unit_train, row_mask, everyone, 256)
+    chip = lax.axis_index("ex")
+    depth = (chip // 16 + jnp.array(RING8, jnp.int32)) % 8
+    own, oth, late = early_score(lay[None], unit_train, row_mask, d_blocks[:3], c_blocks)
     recv = other(oth)
-    tile = 128
-    at = jnp.arange(tile, dtype=jnp.int32)
-    base = (at // mine) * val_ex + at % mine
-    target = jnp.concatenate([base + lay * mine, base + (1 - lay) * mine])
-    spread = (target[:, None] == jnp.arange(2 * tile, dtype=jnp.int32)[None, :]).astype(
-        jnp.bfloat16
-    )
-    return place(own, recv, spread, tile)[:, None, :]
+    own2, oth2 = late_score(lay[None], unit_train, row_mask, *d_blocks[3:], late)
+    recv2 = other(oth2)
+    target = spread_targets(lay, chip, mine)
+    spread = (target[:, :, None] == jnp.arange(512, dtype=jnp.int32)).astype(jnp.bfloat16)
+    return place(depth, own, recv, own2, recv2, spread)[:, None, :]
 
 
 def solution(mesh):

time: 189 us -> 128 us (0.68)
  waiting for transfers between devices: 128 us -> 29.1 us
  starting transfers between devices: 4.83 us -> 49.2 us
  between operations: 13.4 us -> 0.49 us
  local copies, waits for them, and re-layouts: 3.4 us -> 7.76 us
  Pallas kernels: 24.9 us -> 27.2 us
    all_gather x1 -> x0, waiting for transfers between devices: 125 us -> none  [local(): everyone = lax.all_gather(payload, 'ex', axis=0, tiled=True)]
    ppermute x0 -> x29, starting transfers between devices: none -> 39.7 us  [send(): return lax.ppermute(block, ('layer', 'ex'), pairs)]
    ppermute x0 -> x29, waiting for transfers between devices: none -> 28.5 us  [send(): return lax.ppermute(block, ('layer', 'ex'), pairs)]
    ppermute x4 -> x5, starting transfers between devices: 4.83 us -> 9.5 us  [other(): return lax.ppermute(x, 'layer', SWAP)]
    unnamed x6 -> x55, local copies, waits for them, and re-layouts: 2.6 us -> 5.61 us
    ppermute x4 -> x5, waiting for transfers between devices: 3.17 us -> 0.59 us  [other(): return lax.ppermute(x, 'layer', SWAP)]
    pallas_call x2 -> x3, Pallas kernels: 22.5 us -> 24.9 us  [the longest x1 14 us: early_score(): pl.pallas_call(early_kernel, grid_spec=pltpu.PrefetchScalarGridSpec(num_s...]
  transfers between devices with their start and end apart: 5 -> 34, of which waited for: 4 -> 9; matrix products, arithmetic and copies ran while one was open for 7% -> 12% of each run, Pallas kernels for 0% -> 17%
where the time goes in v2:
time: 128 us; the launch traced here: 127 us
  starting transfers between devices  49.2 us (38%)
  waiting for transfers between devices  29.1 us (23%)
  Pallas kernels  27.2 us (21%)
  other arithmetic  12.4 us (10%)
  local copies, waits for them, and re-layouts  7.76 us (6%)
    ppermute x29, starting transfers between devices, send(): return lax.ppermute(block, ('layer', 'ex'), pairs)  39.7 us
    ppermute x29, waiting for transfers between devices, send(): return lax.ppermute(block, ('layer', 'ex'), pairs)  28.5 us
    pallas_call x1, Pallas kernels, early_score(): pl.pallas_call(early_kernel, grid_spec=pltpu.PrefetchScalarGridSpec(num_s...  14 us
    ppermute x5, starting transfers between devices, other(): return lax.ppermute(x, 'layer', SWAP)  9.5 us
    unnamed x55, local copies, waits for them, and re-layouts  5.61 us
    pallas_call x1, Pallas kernels, late_score(): pl.pallas_call(late_kernel, in_specs=[smem] + [vmem] * 5, out_specs=[vmem...  5.58 us
    pallas_call x1, Pallas kernels, place(): pl.pallas_call(place_kernel, in_specs=[pl.BlockSpec(memory_space=pltpu.SM...  5.33 us
    convert_element_type x1, other arithmetic, unit_rows(): (values * (scale_factor * lax.rsqrt(total_sq + 1e-06))[None, :, None]).as...  4.93 us
  transfers between devices with their start and end apart: 34, of which 9 were waited for; matrix products, arithmetic and copies ran while one was open for 12% of the time, Pallas kernels for 17%

profile of v2, /device:TPU:1, one launch (start us, length us, event | category | flops | bytes accessed | tf_op | source)
XLA Modules:
  0.0 127.0 jit_solution(15453735140437918042)
XLA Ops:
  0.0 3.2 %collective-permute-start.1 = (bf16[6,512,256]{2,1,0:T(8,128)(2,1)}, bf16[6,512,256]{2,1,0:T(8,128)(2,1)S(1)}, u32[]{:S(2)}, u32[]{:S(2)}) collective-permute-start(bf16[6,512,256]{2,1,0:T(8,128)(2,1)} %param.10), channel_id=1, source_target_pairs={{0,128},{128,0},{1,129},{129,1},{2,130},{130,2},{3,131},{131,3},{4... | collective-permute-start | bytes 4718600 | tf_op jit(solution)/shard_map/ppermute | solution.py:14
  3.2 0.8 constant_dynamic-slice_fusion
  4.1 0.7 pad_maximum_fusion.2
  4.8 0.5 collective-permute-start.2
  5.3 0.7 convert_element_type.20
  6.0 0.4 collective-permute-done.recv_ref
  6.4 0.6 copy-done.7
  7.0 2.3 %pack.1 = bf16[16,3200]{1,0:T(8,128)(2,1)} custom-call(s32[1]{0:T(128)} %bitcast.lay_ref.s_ref, s32[32]{0:T(128)} %pair_ref.1, bf16[6,32,256]{2,1,0:T(8,128)(2,1)} %val_ref.1, bf16[6,16,256]{2,1,0:T(8,128)(2,1)} %copy-done.7), custom_call_target="tpu_custom_call" | custom-call | tf_op jit(solution)/shard_map/pack/pallas_call | solution.py:51
  9.3 0.8 fusion.29
  10.1 2.7 %collective-permute-start.17 = (bf16[16,1152]{1,0:T(8,128)(2,1)S(1)}, bf16[16,1152]{1,0:T(8,128)(2,1)S(1)}, u32[]{:S(2)}, u32[]{:S(2)}) collective-permute-start(bf16[16,1152]{1,0:T(8,128)(2,1)S(1)} %get-tuple-element.25), channel_id=1, source_target_pairs={{0,3},{1,0},{2,1},{3,2},{4,7},{5,4},{6,5},{7,6},{8,11},{9,8},{10,9... | collective-permute-start | bytes 110600 | tf_op jit(solution)/shard_map/ppermute | solution.py:88
  12.8 0.9 constant_dynamic-update-slice_fusion.8
  13.7 1.7 %collective-permute-start.3 = (bf16[16,2048]{1,0:T(8,128)(2,1)S(1)}, bf16[16,2048]{1,0:T(8,128)(2,1)S(1)}, u32[]{:S(2)}, u32[]{:S(2)}) collective-permute-start(bf16[16,2048]{1,0:T(8,128)(2,1)S(1)} %get-tuple-element.29), channel_id=1, source_target_pairs={{0,16},{1,17},{2,18},{3,19},{4,20},{5,21},{6,22},{7,23},{8,24},{9,... | collective-permute-start | bytes 196616 | tf_op jit(solution)/shard_map/ppermute | solution.py:88
  15.4 4.0 %collective-permute-start.4 = (bf16[16,2048]{1,0:T(8,128)(2,1)S(1)}, bf16[16,2048]{1,0:T(8,128)(2,1)S(1)}, u32[]{:S(2)}, u32[]{:S(2)}) collective-permute-start(bf16[16,2048]{1,0:T(8,128)(2,1)S(1)} %get-tuple-element.29), channel_id=1, source_target_pairs={{0,112},{1,113},{2,114},{3,115},{4,116},{5,117},{6,118},{7,119},{8... | collective-permute-start | bytes 196616 | tf_op jit(solution)/shard_map/ppermute | solution.py:88
  19.4 1.3 %collective-permute-start.19 = (bf16[64,1152]{1,0:T(8,128)(2,1)S(1)}, bf16[64,1152]{1,0:T(8,128)(2,1)S(1)}, u32[]{:S(2)}, u32[]{:S(2)}) collective-permute-start(bf16[64,1152]{1,0:T(8,128)(2,1)S(1)} %pad_maximum_fusion), channel_id=1, source_target_pairs={{0,4},{1,5},{2,6},{3,7},{4,8},{5,9},{6,10},{7,11},{8,12},{9,13},{1... | collective-permute-start | bytes 442376 | tf_op jit(solution)/shard_map/ppermute | solution.py:88
  20.7 1.5 %collective-permute-start.20 = (bf16[64,1152]{1,0:T(8,128)(2,1)S(1)}, bf16[64,1152]{1,0:T(8,128)(2,1)S(1)}, u32[]{:S(2)}, u32[]{:S(2)}) collective-permute-start(bf16[64,1152]{1,0:T(8,128)(2,1)S(1)} %pad_maximum_fusion), channel_id=1, source_target_pairs={{0,12},{1,13},{2,14},{3,15},{4,0},{5,1},{6,2},{7,3},{8,4},{9,5},{1... | collective-permute-start | bytes 442376 | tf_op jit(solution)/shard_map/ppermute | solution.py:88
  22.2 1.5 %collective-permute-start.21 = (bf16[64,1152]{1,0:T(8,128)(2,1)S(1)}, bf16[64,1152]{1,0:T(8,128)(2,1)S(1)}, u32[]{:S(2)}, u32[]{:S(2)}) collective-permute-start(bf16[64,1152]{1,0:T(8,128)(2,1)S(1)} %pad_maximum_fusion), channel_id=1, source_target_pairs={{0,8},{1,9},{2,10},{3,11},{4,12},{5,13},{6,14},{7,15},{8,0},{9,1},... | collective-permute-start | bytes 442376 | tf_op jit(solution)/shard_map/ppermute | solution.py:88
  23.8 0.1 collective-permute-start.5
  23.9 2.7 %collective-permute-start.6 = (bf16[16,2048]{1,0:T(8,128)(2,1)S(1)}, bf16[16,2048]{1,0:T(8,128)(2,1)S(1)}, u32[]{:S(2)}, u32[]{:S(2)}) collective-permute-start(bf16[16,2048]{1,0:T(8,128)(2,1)S(1)} %collective-permute-done.4), channel_id=1, source_target_pairs={{0,112},{1,113},{2,114},{3,115},{4,116},{5,117},{6,118},{7,119},{8... | collective-permute-start | bytes 196616 | tf_op jit(solution)/shard_map/ppermute | solution.py:88
  26.6 1.6 %collective-permute-done.5 = bf16[16,2048]{1,0:T(8,128)(2,1)S(1)} collective-permute-done((bf16[16,2048]{1,0:T(8,128)(2,1)S(1)}, bf16[16,2048]{1,0:T(8,128)(2,1)S(1)}, u32[]{:S(2)}, u32[]{:S(2)}) %collective-permute-start.5) | collective-permute-done | bytes 65568 | tf_op jit(solution)/shard_map/ppermute | solution.py:88
  28.2 3.0 %collective-permute-start.8 = (bf16[16,2048]{1,0:T(8,128)(2,1)S(1)}, bf16[16,2048]{1,0:T(8,128)(2,1)S(1)}, u32[]{:S(2)}, u32[]{:S(2)}) collective-permute-start(bf16[16,2048]{1,0:T(8,128)(2,1)S(1)} %collective-permute-done.6), channel_id=1, source_target_pairs={{0,112},{1,113},{2,114},{3,115},{4,116},{5,117},{6,118},{7,119},{8... | collective-permute-start | bytes 196616 | tf_op jit(solution)/shard_map/ppermute | solution.py:88
  31.3 0.1 collective-permute-start.22
  31.4 2.7 %collective-permute-start.23 = (bf16[256,1152]{1,0:T(8,128)(2,1)S(1)}, bf16[256,1152]{1,0:T(8,128)(2,1)S(1)}, u32[]{:S(2)}, u32[]{:S(2)}) collective-permute-start(bf16[256,1152]{1,0:T(8,128)(2,1)S(1)} %constant_dynamic-update-slice_fusion.21.refs_3_), channel_id=1, source_target_pairs={{0,112},{1,113},{2,114},{3,115},{4,116},{5,117},{6,118},{7,119},{8... | collective-permute-start | bytes 1769480 | tf_op jit(solution)/shard_map/ppermute | solution.py:88
  34.1 2.7 %collective-permute-start.10 = (bf16[8,2048]{1,0:T(8,128)(2,1)S(1)}, bf16[8,2048]{1,0:T(8,128)(2,1)S(1)}, u32[]{:S(2)}, u32[]{:S(2)}) collective-permute-start(bf16[8,2048]{1,0:T(8,128)(2,1)S(1)} %slice.65), channel_id=1, source_target_pairs={{0,112},{1,113},{2,114},{3,115},{4,116},{5,117},{6,118},{7,119},{8... | collective-permute-start | bytes 98312 | tf_op jit(solution)/shard_map/ppermute | solution.py:88
  36.8 9.0 %collective-permute-done.9 = bf16[8,2048]{1,0:T(8,128)(2,1)S(1)} collective-permute-done((bf16[8,2048]{1,0:T(8,128)(2,1)S(1)}, bf16[8,2048]{1,0:T(8,128)(2,1)S(1)}, u32[]{:S(2)}, u32[]{:S(2)}) %collective-permute-start.9) | collective-permute-done | bytes 32800 | tf_op jit(solution)/shard_map/ppermute | solution.py:88
  45.8 0.1 collective-permute-start.11
  45.9 0.9 convolution_convert_fusion.m_ref
  46.8 2.6 %collective-permute-start.12 = (bf16[128,2048]{1,0:T(8,128)(2,1)S(1)}, bf16[128,2048]{1,0:T(8,128)(2,1)S(1)}, u32[]{:S(2)}, u32[]{:S(2)}) collective-permute-start(bf16[128,2048]{1,0:T(8,128)(2,1)S(1)} %get-tuple-element.42), channel_id=1, source_target_pairs={{0,3},{1,0},{2,1},{3,2},{4,7},{5,4},{6,5},{7,6},{8,11},{9,8},{10,9... | collective-permute-start | bytes 1572872 | tf_op jit(solution)/shard_map/ppermute | solution.py:88
  49.5 0.1 collective-permute-start.13
  49.6 0.1 collective-permute-start.24
  49.7 2.6 %collective-permute-start.25 = (bf16[256,1152]{1,0:T(8,128)(2,1)S(1)}, bf16[256,1152]{1,0:T(8,128)(2,1)S(1)}, u32[]{:S(2)}, u32[]{:S(2)}) collective-permute-start(bf16[256,1152]{1,0:T(8,128)(2,1)S(1)} %collective-permute-done.23.refs_5_), channel_id=1, source_target_pairs={{0,112},{1,113},{2,114},{3,115},{4,116},{5,117},{6,118},{7,119},{8... | collective-permute-start | bytes 1769480 | tf_op jit(solution)/shard_map/ppermute | solution.py:88
  52.4 8.7 %collective-permute-done.11 = bf16[128,2048]{1,0:T(8,128)(2,1)S(1)} collective-permute-done((bf16[128,2048]{1,0:T(8,128)(2,1)S(1)}, bf16[128,2048]{1,0:T(8,128)(2,1)S(1)}, u32[]{:S(2)}, u32[]{:S(2)}) %collective-permute-start.11) | collective-permute-done | bytes 524320 | tf_op jit(solution)/shard_map/ppermute | solution.py:88
  61.1 0.1 collective-permute-done.12
  61.3 0.4 collective-permute-start.14
  61.7 2.4 %collective-permute-start.15 = (bf16[512,2048]{1,0:T(8,128)(2,1)S(1)}, bf16[512,2048]{1,0:T(8,128)(2,1)S(1)}, u32[]{:S(2)}, u32[]{:S(2)}) collective-permute-start(bf16[512,2048]{1,0:T(8,128)(2,1)S(1)} %constant_dynamic-update-slice_fusion.9), channel_id=1, source_target_pairs={{0,12},{1,13},{2,14},{3,15},{4,0},{5,1},{6,2},{7,3},{8,4},{9,5},{1... | collective-permute-start | bytes 6291464 | tf_op jit(solution)/shard_map/ppermute | solution.py:88
  64.1 2.7 %collective-permute-start.27 = (bf16[256,1152]{1,0:T(8,128)(2,1)S(1)}, bf16[256,1152]{1,0:T(8,128)(2,1)S(1)}, u32[]{:S(2)}, u32[]{:S(2)}) collective-permute-start(bf16[256,1152]{1,0:T(8,128)(2,1)S(1)} %collective-permute-done.25.refs_7_), channel_id=1, source_target_pairs={{0,112},{1,113},{2,114},{3,115},{4,116},{5,117},{6,118},{7,119},{8... | collective-permute-start | bytes 1769480 | tf_op jit(solution)/shard_map/ppermute | solution.py:88
  66.8 3.8 %multiply_reduce_fusion = f32[512]{0:T(512)S(1)} fusion(f32[12,256]{1,0:T(8,128)S(1)} %get-tuple-element.47, bf16[6,512,256]{2,1,0:T(8,128)(2,1)S(1)} %collective-permute-done.1, bf16[6,512,256]{2,1,0:T(8,128)(2,1)S(1)} %copy-done, f32[12,256]{1,0:T(8,128)S(1)} %get-tuple-element.46), kind=kLoop, calls=%fused_computation.8 | loop fusion | flops 17300992 | bytes 3172352 | tf_op jit(solution)/shard_map/reduce_sum | solution.py:24
  70.6 3.7 %collective-permute-done.26.refs_8_ = bf16[256,1152]{1,0:T(8,128)(2,1)S(1)} collective-permute-done((bf16[256,1152]{1,0:T(8,128)(2,1)S(1)}, bf16[256,1152]{1,0:T(8,128)(2,1)S(1)}, u32[]{:S(2)}, u32[]{:S(2)}) %collective-permute-start.26) | collective-permute-done | bytes 589856 | tf_op jit(solution)/shard_map/ppermute | solution.py:88
  74.3 0.1 collective-permute-start.28
  74.4 0.7 copy-done.5
  75.2 0.8 copy-done.6
  75.9 2.0 %collective-permute-start.29 = (bf16[128,1152]{1,0:T(8,128)(2,1)S(1)}, bf16[128,1152]{1,0:T(8,128)(2,1)S(1)}, u32[]{:S(2)}, u32[]{:S(2)}) collective-permute-start(bf16[128,1152]{1,0:T(8,128)(2,1)S(1)} %slice.67), channel_id=1, source_target_pairs={{0,112},{1,113},{2,114},{3,115},{4,116},{5,117},{6,118},{7,119},{8... | collective-permute-start | bytes 884744 | tf_op jit(solution)/shard_map/ppermute | solution.py:88
  77.9 4.9 %multiply_convert_fusion.a_ref = bf16[12,512,256]{2,1,0:T(8,128)(2,1)} fusion(f32[512]{0:T(512)S(1)} %rsqrt_multiply_fusion, f32[12,256]{1,0:T(8,128)S(1)} %get-tuple-element.47, bf16[6,512,256]{2,1,0:T(8,128)(2,1)S(1)} %collective-permute-done.1, bf16[6,512,256]{2,1,0:T(8,128)(2,1)S(1)} %copy-done, f32[12,256]{1,0:T(8,128)S(1)} %get-tuple-element.46), kind=kLoop, calls=%fused_computation.7 | loop fusion | flops 17301504 | bytes 6318080 | tf_op jit(solution)/shard_map/convert_element_type | solution.py:25
  82.8 5.1 %collective-permute-done.14 = bf16[512,2048]{1,0:T(8,128)(2,1)S(1)} collective-permute-done((bf16[512,2048]{1,0:T(8,128)(2,1)S(1)}, bf16[512,2048]{1,0:T(8,128)(2,1)S(1)}, u32[]{:S(2)}, u32[]{:S(2)}) %collective-permute-start.14) | collective-permute-done | bytes 2097184 | tf_op jit(solution)/shard_map/ppermute | solution.py:88
  87.9 0.1 slice.68
  88.0 0.1 collective-permute-start.31
  88.1 0.3 collective-permute-done.15
  88.4 0.1 slice.69
  88.5 0.8 copy-done.2
  89.3 2.7 %collective-permute-start.32 = (bf16[256,2048]{1,0:T(8,128)(2,1)S(1)}, bf16[256,2048]{1,0:T(8,128)(2,1)}, u32[]{:S(2)}, u32[]{:S(2)}) collective-permute-start(bf16[256,2048]{1,0:T(8,128)(2,1)S(1)} %slice.69), channel_id=1, source_target_pairs={{0,12},{1,13},{2,14},{3,15},{4,0},{5,1},{6,2},{7,3},{8,4},{9,5},{1... | collective-permute-start | bytes 3145736 | tf_op jit(solution)/shard_map/ppermute | solution.py:88
  92.0 0.8 copy-done.18
  92.7 0.1 copy-done.17
  92.8 14.0 %early_score.1 = (bf16[256,2048]{1,0:T(8,128)(2,1)}, bf16[256,2048]{1,0:T(8,128)(2,1)}, bf16[512,1152]{1,0:T(8,128)(2,1)}) custom-call(s32[1]{0:T(128)} %bitcast.lay_ref.s_ref, bf16[12,512,256]{2,1,0:T(8,128)(2,1)} %multiply_convert_fusion.a_ref, bf16[512,128]{1,0:T(8,128)(2,1)} %convolution_convert_fusion.m_ref, bf16[4,8,16,2048]{3,2,1,0:T(8,128)(2,1)} %bitcast.28, ...), custom_call_target="tpu_custom_call" | custom-call | flops 4831838208 | bytes 31457280 | tf_op jit(solution)/shard_map/early_score/pallas_call | solution.py:166
  106.8 5.7 %collective-permute-start.30 = (bf16[256,2048]{1,0:T(8,128)(2,1)}, bf16[256,2048]{1,0:T(8,128)(2,1)S(1)}, u32[]{:S(2)}, u32[]{:S(2)}) collective-permute-start(bf16[256,2048]{1,0:T(8,128)(2,1)} %get-tuple-element.17), channel_id=1, source_target_pairs={{0,128},{128,0},{1,129},{129,1},{2,130},{130,2},{3,131},{131,3},{4... | collective-permute-start | bytes 3145736 | tf_op jit(solution)/shard_map/ppermute | solution.py:14
  112.6 0.1 slice.51
  112.7 0.1 slice.50
  112.7 0.1 concatenate.32
  112.8 0.1 concatenate.33
  113.0 0.6 and_select_fusion.8.depth_ref
  113.5 5.6 %late_score.1 = (bf16[256,512]{1,0:T(8,128)(2,1)}, bf16[256,512]{1,0:T(8,128)(2,1)}) custom-call(s32[1]{0:T(128)} %bitcast.lay_ref.s_ref, bf16[12,512,256]{2,1,0:T(8,128)(2,1)} %multiply_convert_fusion.a_ref, bf16[512,128]{1,0:T(8,128)(2,1)} %convolution_convert_fusion.m_ref, bf16[2,8,16,2048]{3,2,1,0:T(8,128)(2,1)} %bitcast.8.near_ref, ...), custom_call_target="tpu_custom_call" | custom-call | tf_op jit(solution)/shard_map/late_score/pallas_call | solution.py:201
  119.2 1.5 %fusion.5.spread_ref = bf16[2,768,512]{2,1,0:T(8,128)(2,1)} fusion(s32[2,768]{1,0:T(2,128)S(1)} %pad_add_fusion), kind=kLoop, calls=%fused_computation.10 | loop fusion | flops 1572864 | bytes 1579008 | tf_op jit(solution)/shard_map/convert_element_type | solution.py:312
  120.6 0.2 collective-permute-done.33.recv2_ref
  120.9 0.8 copy-done.1
  121.6 0.1 copy-done.4
  121.7 5.3 %place.1 = bf16[256,4096]{1,0:T(8,128)(2,1)} custom-call(s32[8]{0:T(128)} %and_select_fusion.8.depth_ref, bf16[256,2048]{1,0:T(8,128)(2,1)} %get-tuple-element.16.own_ref, bf16[256,2048]{1,0:T(8,128)(2,1)} %copy-done.1, bf16[256,512]{1,0:T(8,128)(2,1)} %get-tuple-element.19.own2_ref, bf16[256,512]{1,0:T(8,128)(2,1)} %copy-done.4, ...), custom_call_target="tpu_custom_call" | custom-call | tf_op jit(solution)/shard_map/place/pallas_call | solution.py:228
  (98 shorter events, 0.7 us)
Async XLA Ops:
  0.0 49.5 %copy-start.9 = (f32[6,256]{1,0:T(8,128)S(1)}, f32[6,256]{1,0:T(8,128)}, u32[]{:S(2)}) copy-start(f32[6,256]{1,0:T(8,128)} %param.12) | copy-start | bytes 18436
  0.0 49.5 %copy-start.8 = (f32[6,256]{1,0:T(8,128)S(1)}, f32[6,256]{1,0:T(8,128)}, u32[]{:S(2)}) copy-start(f32[6,256]{1,0:T(8,128)} %param.13) | copy-start | bytes 18436
  0.0 45.9 %copy-start.11 = (s32[512]{0:T(512)S(1)}, s32[512]{0:T(512)}, u32[]{:S(2)}) copy-start(s32[512]{0:T(512)} %param.14) | copy-start | bytes 6148
  0.0 9.3 %collective-permute-start.1 = (bf16[6,512,256]{2,1,0:T(8,128)(2,1)}, bf16[6,512,256]{2,1,0:T(8,128)(2,1)S(1)}, u32[]{:S(2)}, u32[]{:S(2)}) collective-permute-start(bf16[6,512,256]{2,1,0:T(8,128)(2,1)} %param.10), channel_id=1, source_target_pairs={{0,128},{128,0},{1,129},{129,1},{2,130},{130,2},{3,131},{131,3},{4... | collective-permute-start | bytes 4718600 | tf_op jit(solution)/shard_map/ppermute | solution.py:14
  4.1 2.3 %collective-permute-start = (bf16[6,16,256]{2,1,0:T(8,128)(2,1)S(1)}, bf16[6,16,256]{2,1,0:T(8,128)(2,1)S(1)}, u32[]{:S(2)}, u32[]{:S(2)}) collective-permute-start(bf16[6,16,256]{2,1,0:T(8,128)(2,1)S(1)} %constant_dynamic-slice_fusion), channel_id=1, source_target_pairs={{0,128},{128,0},{1,129},{129,1},{2,130},{130,2},{3,131},{131,3},{4... | collective-permute-start | bytes 147464 | tf_op jit(solution)/shard_map/ppermute | solution.py:14
  4.8 4.5 %collective-permute-start.2 = (f32[2,6,256]{2,1,0:T(8,128)S(1)}, f32[2,6,256]{2,1,0:T(8,128)S(1)}, u32[]{:S(2)}, u32[]{:S(2)}) collective-permute-start(f32[2,6,256]{2,1,0:T(8,128)S(1)} %pad_maximum_fusion.2), channel_id=1, source_target_pairs={{0,128},{128,0},{1,129},{129,1},{2,130},{130,2},{3,131},{131,3},{4... | collective-permute-start | bytes 36872 | tf_op jit(solution)/shard_map/ppermute | solution.py:14
  6.4 0.6 copy-start.7
  10.1 9.3 %collective-permute-start.16 = (bf16[16,1152]{1,0:T(8,128)(2,1)S(1)}, bf16[16,1152]{1,0:T(8,128)(2,1)S(1)}, u32[]{:S(2)}, u32[]{:S(2)}) collective-permute-start(bf16[16,1152]{1,0:T(8,128)(2,1)S(1)} %get-tuple-element.25), channel_id=1, source_target_pairs={{0,1},{1,2},{2,3},{3,0},{4,5},{5,6},{6,7},{7,4},{8,9},{9,10},{10,1... | collective-permute-start | bytes 110600 | tf_op jit(solution)/shard_map/ppermute | solution.py:88
  10.1 9.3 %collective-permute-start.17 = (bf16[16,1152]{1,0:T(8,128)(2,1)S(1)}, bf16[16,1152]{1,0:T(8,128)(2,1)S(1)}, u32[]{:S(2)}, u32[]{:S(2)}) collective-permute-start(bf16[16,1152]{1,0:T(8,128)(2,1)S(1)} %get-tuple-element.25), channel_id=1, source_target_pairs={{0,3},{1,0},{2,1},{3,2},{4,7},{5,4},{6,5},{7,6},{8,11},{9,8},{10,9... | collective-permute-start | bytes 110600 | tf_op jit(solution)/shard_map/ppermute | solution.py:88
  12.7 6.7 %collective-permute-start.18 = (bf16[16,1152]{1,0:T(8,128)(2,1)S(1)}, bf16[16,1152]{1,0:T(8,128)(2,1)S(1)}, u32[]{:S(2)}, u32[]{:S(2)}) collective-permute-start(bf16[16,1152]{1,0:T(8,128)(2,1)S(1)} %get-tuple-element.25), channel_id=1, source_target_pairs={{0,2},{1,3},{2,0},{3,1},{4,6},{5,7},{6,4},{7,5},{8,10},{9,11},{10,... | collective-permute-start | bytes 110600 | tf_op jit(solution)/shard_map/ppermute | solution.py:88
  13.7 10.1 %collective-permute-start.3 = (bf16[16,2048]{1,0:T(8,128)(2,1)S(1)}, bf16[16,2048]{1,0:T(8,128)(2,1)S(1)}, u32[]{:S(2)}, u32[]{:S(2)}) collective-permute-start(bf16[16,2048]{1,0:T(8,128)(2,1)S(1)} %get-tuple-element.29), channel_id=1, source_target_pairs={{0,16},{1,17},{2,18},{3,19},{4,20},{5,21},{6,22},{7,23},{8,24},{9,... | collective-permute-start | bytes 196616 | tf_op jit(solution)/shard_map/ppermute | solution.py:88
  15.4 8.5 %collective-permute-start.4 = (bf16[16,2048]{1,0:T(8,128)(2,1)S(1)}, bf16[16,2048]{1,0:T(8,128)(2,1)S(1)}, u32[]{:S(2)}, u32[]{:S(2)}) collective-permute-start(bf16[16,2048]{1,0:T(8,128)(2,1)S(1)} %get-tuple-element.29), channel_id=1, source_target_pairs={{0,112},{1,113},{2,114},{3,115},{4,116},{5,117},{6,118},{7,119},{8... | collective-permute-start | bytes 196616 | tf_op jit(solution)/shard_map/ppermute | solution.py:88
  19.4 11.7 %collective-permute-start.19 = (bf16[64,1152]{1,0:T(8,128)(2,1)S(1)}, bf16[64,1152]{1,0:T(8,128)(2,1)S(1)}, u32[]{:S(2)}, u32[]{:S(2)}) collective-permute-start(bf16[64,1152]{1,0:T(8,128)(2,1)S(1)} %pad_maximum_fusion), channel_id=1, source_target_pairs={{0,4},{1,5},{2,6},{3,7},{4,8},{5,9},{6,10},{7,11},{8,12},{9,13},{1... | collective-permute-start | bytes 442376 | tf_op jit(solution)/shard_map/ppermute | solution.py:88
  20.7 10.5 %collective-permute-start.20 = (bf16[64,1152]{1,0:T(8,128)(2,1)S(1)}, bf16[64,1152]{1,0:T(8,128)(2,1)S(1)}, u32[]{:S(2)}, u32[]{:S(2)}) collective-permute-start(bf16[64,1152]{1,0:T(8,128)(2,1)S(1)} %pad_maximum_fusion), channel_id=1, source_target_pairs={{0,12},{1,13},{2,14},{3,15},{4,0},{5,1},{6,2},{7,3},{8,4},{9,5},{1... | collective-permute-start | bytes 442376 | tf_op jit(solution)/shard_map/ppermute | solution.py:88
  22.2 9.1 %collective-permute-start.21 = (bf16[64,1152]{1,0:T(8,128)(2,1)S(1)}, bf16[64,1152]{1,0:T(8,128)(2,1)S(1)}, u32[]{:S(2)}, u32[]{:S(2)}) collective-permute-start(bf16[64,1152]{1,0:T(8,128)(2,1)S(1)} %pad_maximum_fusion), channel_id=1, source_target_pairs={{0,8},{1,9},{2,10},{3,11},{4,12},{5,13},{6,14},{7,15},{8,0},{9,1},... | collective-permute-start | bytes 442376 | tf_op jit(solution)/shard_map/ppermute | solution.py:88
  23.8 4.4 %collective-permute-start.5 = (bf16[16,2048]{1,0:T(8,128)(2,1)S(1)}, bf16[16,2048]{1,0:T(8,128)(2,1)S(1)}, u32[]{:S(2)}, u32[]{:S(2)}) collective-permute-start(bf16[16,2048]{1,0:T(8,128)(2,1)S(1)} %collective-permute-done.3), channel_id=1, source_target_pairs={{0,16},{1,17},{2,18},{3,19},{4,20},{5,21},{6,22},{7,23},{8,24},{9,... | collective-permute-start | bytes 196616 | tf_op jit(solution)/shard_map/ppermute | solution.py:88
  23.9 4.3 %collective-permute-start.6 = (bf16[16,2048]{1,0:T(8,128)(2,1)S(1)}, bf16[16,2048]{1,0:T(8,128)(2,1)S(1)}, u32[]{:S(2)}, u32[]{:S(2)}) collective-permute-start(bf16[16,2048]{1,0:T(8,128)(2,1)S(1)} %collective-permute-done.4), channel_id=1, source_target_pairs={{0,112},{1,113},{2,114},{3,115},{4,116},{5,117},{6,118},{7,119},{8... | collective-permute-start | bytes 196616 | tf_op jit(solution)/shard_map/ppermute | solution.py:88
  28.2 5.9 %collective-permute-start.7 = (bf16[16,2048]{1,0:T(8,128)(2,1)S(1)}, bf16[16,2048]{1,0:T(8,128)(2,1)S(1)}, u32[]{:S(2)}, u32[]{:S(2)}) collective-permute-start(bf16[16,2048]{1,0:T(8,128)(2,1)S(1)} %collective-permute-done.5), channel_id=1, source_target_pairs={{0,16},{1,17},{2,18},{3,19},{4,20},{5,21},{6,22},{7,23},{8,24},{9,... | collective-permute-start | bytes 196616 | tf_op jit(solution)/shard_map/ppermute | solution.py:88
  28.2 5.9 %collective-permute-start.8 = (bf16[16,2048]{1,0:T(8,128)(2,1)S(1)}, bf16[16,2048]{1,0:T(8,128)(2,1)S(1)}, u32[]{:S(2)}, u32[]{:S(2)}) collective-permute-start(bf16[16,2048]{1,0:T(8,128)(2,1)S(1)} %collective-permute-done.6), channel_id=1, source_target_pairs={{0,112},{1,113},{2,114},{3,115},{4,116},{5,117},{6,118},{7,119},{8... | collective-permute-start | bytes 196616 | tf_op jit(solution)/shard_map/ppermute | solution.py:88
  31.3 29.7 %copy-start.10 = (bf16[256,1152]{1,0:T(8,128)(2,1)}, bf16[256,1152]{1,0:T(8,128)(2,1)S(1)}, u32[]{:S(2)}) copy-start(bf16[256,1152]{1,0:T(8,128)(2,1)S(1)} %constant_dynamic-update-slice_fusion.21.refs_3_) | copy-start | bytes 1769476
  31.3 35.5 %copy-start = (bf16[6,512,256]{2,1,0:T(8,128)(2,1)S(1)}, bf16[6,512,256]{2,1,0:T(8,128)(2,1)}, u32[]{:S(2)}) copy-start(bf16[6,512,256]{2,1,0:T(8,128)(2,1)} %param.10) | copy-start | bytes 4718596
  31.3 18.3 %collective-permute-start.22 = (bf16[256,1152]{1,0:T(8,128)(2,1)S(1)}, bf16[256,1152]{1,0:T(8,128)(2,1)S(1)}, u32[]{:S(2)}, u32[]{:S(2)}) collective-permute-start(bf16[256,1152]{1,0:T(8,128)(2,1)S(1)} %constant_dynamic-update-slice_fusion.21.refs_3_), channel_id=1, source_target_pairs={{0,16},{1,17},{2,18},{3,19},{4,20},{5,21},{6,22},{7,23},{8,24},{9,... | collective-permute-start | bytes 1769480 | tf_op jit(solution)/shard_map/ppermute | solution.py:88
  31.4 18.3 %collective-permute-start.23 = (bf16[256,1152]{1,0:T(8,128)(2,1)S(1)}, bf16[256,1152]{1,0:T(8,128)(2,1)S(1)}, u32[]{:S(2)}, u32[]{:S(2)}) collective-permute-start(bf16[256,1152]{1,0:T(8,128)(2,1)S(1)} %constant_dynamic-update-slice_fusion.21.refs_3_), channel_id=1, source_target_pairs={{0,112},{1,113},{2,114},{3,115},{4,116},{5,117},{6,118},{7,119},{8... | collective-permute-start | bytes 1769480 | tf_op jit(solution)/shard_map/ppermute | solution.py:88
  34.1 11.7 %collective-permute-start.9 = (bf16[8,2048]{1,0:T(8,128)(2,1)S(1)}, bf16[8,2048]{1,0:T(8,128)(2,1)S(1)}, u32[]{:S(2)}, u32[]{:S(2)}) collective-permute-start(bf16[8,2048]{1,0:T(8,128)(2,1)S(1)} %slice.64), channel_id=1, source_target_pairs={{0,16},{1,17},{2,18},{3,19},{4,20},{5,21},{6,22},{7,23},{8,24},{9,... | collective-permute-start | bytes 98312 | tf_op jit(solution)/shard_map/ppermute | solution.py:88
  34.1 11.7 %collective-permute-start.10 = (bf16[8,2048]{1,0:T(8,128)(2,1)S(1)}, bf16[8,2048]{1,0:T(8,128)(2,1)S(1)}, u32[]{:S(2)}, u32[]{:S(2)}) collective-permute-start(bf16[8,2048]{1,0:T(8,128)(2,1)S(1)} %slice.65), channel_id=1, source_target_pairs={{0,112},{1,113},{2,114},{3,115},{4,116},{5,117},{6,118},{7,119},{8... | collective-permute-start | bytes 98312 | tf_op jit(solution)/shard_map/ppermute | solution.py:88
  45.8 15.2 %collective-permute-start.11 = (bf16[128,2048]{1,0:T(8,128)(2,1)S(1)}, bf16[128,2048]{1,0:T(8,128)(2,1)S(1)}, u32[]{:S(2)}, u32[]{:S(2)}) collective-permute-start(bf16[128,2048]{1,0:T(8,128)(2,1)S(1)} %get-tuple-element.42), channel_id=1, source_target_pairs={{0,1},{1,2},{2,3},{3,0},{4,5},{5,6},{6,7},{7,4},{8,9},{9,10},{10,1... | collective-permute-start | bytes 1572872 | tf_op jit(solution)/shard_map/ppermute | solution.py:88
  46.8 14.4 %collective-permute-start.12 = (bf16[128,2048]{1,0:T(8,128)(2,1)S(1)}, bf16[128,2048]{1,0:T(8,128)(2,1)S(1)}, u32[]{:S(2)}, u32[]{:S(2)}) collective-permute-start(bf16[128,2048]{1,0:T(8,128)(2,1)S(1)} %get-tuple-element.42), channel_id=1, source_target_pairs={{0,3},{1,0},{2,1},{3,2},{4,7},{5,4},{6,5},{7,6},{8,11},{9,8},{10,9... | collective-permute-start | bytes 1572872 | tf_op jit(solution)/shard_map/ppermute | solution.py:88
  49.5 11.8 %collective-permute-start.13 = (bf16[128,2048]{1,0:T(8,128)(2,1)S(1)}, bf16[128,2048]{1,0:T(8,128)(2,1)S(1)}, u32[]{:S(2)}, u32[]{:S(2)}) collective-permute-start(bf16[128,2048]{1,0:T(8,128)(2,1)S(1)} %get-tuple-element.42), channel_id=1, source_target_pairs={{0,2},{1,3},{2,0},{3,1},{4,6},{5,7},{6,4},{7,5},{8,10},{9,11},{10,... | collective-permute-start | bytes 1572872 | tf_op jit(solution)/shard_map/ppermute | solution.py:88
  49.6 21.0 %copy-start.13 = (bf16[256,1152]{1,0:T(8,128)(2,1)}, bf16[256,1152]{1,0:T(8,128)(2,1)S(1)}, u32[]{:S(2)}) copy-start(bf16[256,1152]{1,0:T(8,128)(2,1)S(1)} %collective-permute-done.22.refs_4_) | copy-start | bytes 1769476
  49.6 14.5 %collective-permute-start.24 = (bf16[256,1152]{1,0:T(8,128)(2,1)S(1)}, bf16[256,1152]{1,0:T(8,128)(2,1)S(1)}, u32[]{:S(2)}, u32[]{:S(2)}) collective-permute-start(bf16[256,1152]{1,0:T(8,128)(2,1)S(1)} %collective-permute-done.22.refs_4_), channel_id=1, source_target_pairs={{0,16},{1,17},{2,18},{3,19},{4,20},{5,21},{6,22},{7,23},{8,24},{9,... | collective-permute-start | bytes 1769480 | tf_op jit(solution)/shard_map/ppermute | solution.py:88
  49.7 20.9 %copy-start.14 = (bf16[256,1152]{1,0:T(8,128)(2,1)}, bf16[256,1152]{1,0:T(8,128)(2,1)S(1)}, u32[]{:S(2)}) copy-start(bf16[256,1152]{1,0:T(8,128)(2,1)S(1)} %collective-permute-done.23.refs_5_) | copy-start | bytes 1769476
  49.7 14.4 %collective-permute-start.25 = (bf16[256,1152]{1,0:T(8,128)(2,1)S(1)}, bf16[256,1152]{1,0:T(8,128)(2,1)S(1)}, u32[]{:S(2)}, u32[]{:S(2)}) collective-permute-start(bf16[256,1152]{1,0:T(8,128)(2,1)S(1)} %collective-permute-done.23.refs_5_), channel_id=1, source_target_pairs={{0,112},{1,113},{2,114},{3,115},{4,116},{5,117},{6,118},{7,119},{8... | collective-permute-start | bytes 1769480 | tf_op jit(solution)/shard_map/ppermute | solution.py:88
  61.3 13.9 %copy-start.12 = (bf16[512,2048]{1,0:T(8,128)(2,1)}, bf16[512,2048]{1,0:T(8,128)(2,1)S(1)}, u32[]{:S(2)}) copy-start(bf16[512,2048]{1,0:T(8,128)(2,1)S(1)} %constant_dynamic-update-slice_fusion.9) | copy-start | bytes 6291460
  61.3 26.6 %collective-permute-start.14 = (bf16[512,2048]{1,0:T(8,128)(2,1)S(1)}, bf16[512,2048]{1,0:T(8,128)(2,1)S(1)}, u32[]{:S(2)}, u32[]{:S(2)}) collective-permute-start(bf16[512,2048]{1,0:T(8,128)(2,1)S(1)} %constant_dynamic-update-slice_fusion.9), channel_id=1, source_target_pairs={{0,4},{1,5},{2,6},{3,7},{4,8},{5,9},{6,10},{7,11},{8,12},{9,13},{1... | collective-permute-start | bytes 6291464 | tf_op jit(solution)/shard_map/ppermute | solution.py:88
  61.7 26.7 %collective-permute-start.15 = (bf16[512,2048]{1,0:T(8,128)(2,1)S(1)}, bf16[512,2048]{1,0:T(8,128)(2,1)S(1)}, u32[]{:S(2)}, u32[]{:S(2)}) collective-permute-start(bf16[512,2048]{1,0:T(8,128)(2,1)S(1)} %constant_dynamic-update-slice_fusion.9), channel_id=1, source_target_pairs={{0,12},{1,13},{2,14},{3,15},{4,0},{5,1},{6,2},{7,3},{8,4},{9,5},{1... | collective-permute-start | bytes 6291464 | tf_op jit(solution)/shard_map/ppermute | solution.py:88
  64.1 11.1 %copy-start.15 = (bf16[256,1152]{1,0:T(8,128)(2,1)}, bf16[256,1152]{1,0:T(8,128)(2,1)S(1)}, u32[]{:S(2)}) copy-start(bf16[256,1152]{1,0:T(8,128)(2,1)S(1)} %collective-permute-done.24.refs_6_) | copy-start | bytes 1769476
  64.1 10.2 %collective-permute-start.26 = (bf16[256,1152]{1,0:T(8,128)(2,1)S(1)}, bf16[256,1152]{1,0:T(8,128)(2,1)S(1)}, u32[]{:S(2)}, u32[]{:S(2)}) collective-permute-start(bf16[256,1152]{1,0:T(8,128)(2,1)S(1)} %collective-permute-done.24.refs_6_), channel_id=1, source_target_pairs={{0,16},{1,17},{2,18},{3,19},{4,20},{5,21},{6,22},{7,23},{8,24},{9,... | collective-permute-start | bytes 1769480 | tf_op jit(solution)/shard_map/ppermute | solution.py:88
  64.1 11.1 %copy-start.16 = (bf16[256,1152]{1,0:T(8,128)(2,1)}, bf16[256,1152]{1,0:T(8,128)(2,1)S(1)}, u32[]{:S(2)}) copy-start(bf16[256,1152]{1,0:T(8,128)(2,1)S(1)} %collective-permute-done.25.refs_7_) | copy-start | bytes 1769476
  64.1 10.3 %collective-permute-start.27 = (bf16[256,1152]{1,0:T(8,128)(2,1)S(1)}, bf16[256,1152]{1,0:T(8,128)(2,1)S(1)}, u32[]{:S(2)}, u32[]{:S(2)}) collective-permute-start(bf16[256,1152]{1,0:T(8,128)(2,1)S(1)} %collective-permute-done.25.refs_7_), channel_id=1, source_target_pairs={{0,112},{1,113},{2,114},{3,115},{4,116},{5,117},{6,118},{7,119},{8... | collective-permute-start | bytes 1769480 | tf_op jit(solution)/shard_map/ppermute | solution.py:88
  74.3 0.8 copy-start.5
  74.3 17.6 %collective-permute-start.28 = (bf16[128,1152]{1,0:T(8,128)(2,1)S(1)}, bf16[128,1152]{1,0:T(8,128)(2,1)S(1)}, u32[]{:S(2)}, u32[]{:S(2)}) collective-permute-start(bf16[128,1152]{1,0:T(8,128)(2,1)S(1)} %slice.66), channel_id=1, source_target_pairs={{0,16},{1,17},{2,18},{3,19},{4,20},{5,21},{6,22},{7,23},{8,24},{9,... | collective-permute-start | bytes 884744 | tf_op jit(solution)/shard_map/ppermute | solution.py:88
  75.1 0.8 copy-start.6
  75.9 16.0 %collective-permute-start.29 = (bf16[128,1152]{1,0:T(8,128)(2,1)S(1)}, bf16[128,1152]{1,0:T(8,128)(2,1)S(1)}, u32[]{:S(2)}, u32[]{:S(2)}) collective-permute-start(bf16[128,1152]{1,0:T(8,128)(2,1)S(1)} %slice.67), channel_id=1, source_target_pairs={{0,112},{1,113},{2,114},{3,115},{4,116},{5,117},{6,118},{7,119},{8... | collective-permute-start | bytes 884744 | tf_op jit(solution)/shard_map/ppermute | solution.py:88
  87.9 1.3 %copy-start.2 = (bf16[512,2048]{1,0:T(8,128)(2,1)}, bf16[512,2048]{1,0:T(8,128)(2,1)S(1)}, u32[]{:S(2)}) copy-start(bf16[512,2048]{1,0:T(8,128)(2,1)S(1)} %collective-permute-done.14) | copy-start | bytes 6291460
  88.0 25.5 %collective-permute-start.31 = (bf16[256,2048]{1,0:T(8,128)(2,1)S(1)}, bf16[256,2048]{1,0:T(8,128)(2,1)}, u32[]{:S(2)}, u32[]{:S(2)}) collective-permute-start(bf16[256,2048]{1,0:T(8,128)(2,1)S(1)} %slice.68), channel_id=1, source_target_pairs={{0,4},{1,5},{2,6},{3,7},{4,8},{5,9},{6,10},{7,11},{8,12},{9,13},{1... | collective-permute-start | bytes 3145736 | tf_op jit(solution)/shard_map/ppermute | solution.py:88
  88.4 4.3 %copy-start.3 = (bf16[512,2048]{1,0:T(8,128)(2,1)}, bf16[512,2048]{1,0:T(8,128)(2,1)S(1)}, u32[]{:S(2)}) copy-start(bf16[512,2048]{1,0:T(8,128)(2,1)S(1)} %collective-permute-done.15) | copy-start | bytes 6291460
  89.3 24.3 %collective-permute-start.32 = (bf16[256,2048]{1,0:T(8,128)(2,1)S(1)}, bf16[256,2048]{1,0:T(8,128)(2,1)}, u32[]{:S(2)}, u32[]{:S(2)}) collective-permute-start(bf16[256,2048]{1,0:T(8,128)(2,1)S(1)} %slice.69), channel_id=1, source_target_pairs={{0,12},{1,13},{2,14},{3,15},{4,0},{5,1},{6,2},{7,3},{8,4},{9,5},{1... | collective-permute-start | bytes 3145736 | tf_op jit(solution)/shard_map/ppermute | solution.py:88
  92.0 0.8 copy-start.17
  92.0 0.8 copy-start.18
  92.8 20.1 %copy-start.19 = (s32[8]{0:T(128)S(1)}, s32[8]{0:T(128)}, u32[]{:S(2)}) copy-start(s32[8]{0:T(128)} %constant.174.clone) | copy-start | bytes 100
  106.8 13.8 %collective-permute-start.30 = (bf16[256,2048]{1,0:T(8,128)(2,1)}, bf16[256,2048]{1,0:T(8,128)(2,1)S(1)}, u32[]{:S(2)}, u32[]{:S(2)}) collective-permute-start(bf16[256,2048]{1,0:T(8,128)(2,1)} %get-tuple-element.17), channel_id=1, source_target_pairs={{0,128},{128,0},{1,129},{129,1},{2,130},{130,2},{3,131},{131,3},{4... | collective-permute-start | bytes 3145736 | tf_op jit(solution)/shard_map/ppermute | solution.py:14
  119.1 1.7 %collective-permute-start.33 = (bf16[256,512]{1,0:T(8,128)(2,1)}, bf16[256,512]{1,0:T(8,128)(2,1)S(1)}, u32[]{:S(2)}, u32[]{:S(2)}) collective-permute-start(bf16[256,512]{1,0:T(8,128)(2,1)} %get-tuple-element.20), channel_id=1, source_target_pairs={{0,128},{128,0},{1,129},{129,1},{2,130},{130,2},{3,131},{131,3},{4... | collective-permute-start | bytes 786440 | tf_op jit(solution)/shard_map/ppermute | solution.py:14
  120.6 1.0 copy-start.1
  120.9 0.8 copy-start.4
